TPU v7x, 32 devices: a whole 2x2x4 slice. The times are simulated.
32 devices in a mesh: dp: 8 (over y, x, core), mp: 4 (over z).
Axes of the slice: x: 2, y: 2, z: 4, core: 2. Of those that a mesh axis runs over, the one named last changes fastest.
Arguments:
- tokens: bfloat16 [16, 512, 768], P('dp'), may hold values from -6 to 6
- lengths: int32 [16], P('dp'), may hold values from 40 to 512, as said below
- coords: int32 [16, 2, 512], P('dp'), may hold values from 0 to 999
- w_qkv: bfloat16 [3, 768, 768], P(None, None, 'mp'), may hold values from -0.375 to 0.375
- w_pos: bfloat16 [2, 768, 768], P(None, None, 'mp'), may hold values from -0.375 to 0.375
- w_out: bfloat16 [768, 768], P('mp'), may hold values from -0.875 to 0.875
- b_out: float32 [768], replicated, may hold values from -3 to 3
- gain_one: float32 [768], replicated, may hold values from 0.5 to 1.5
- shift_one: float32 [768], replicated, may hold values from -3 to 3
- w_in: bfloat16 [768, 3072], P(None, 'mp'), may hold values from -0.21875 to 0.21875
- b_in: float32 [3072], P('mp'), may hold values from -3 to 3
- w_back: bfloat16 [3072, 768], P('mp'), may hold values from -0.109375 to 0.109375
- b_back: float32 [768], replicated, may hold values from -3 to 3
- gain_two: float32 [768], replicated, may hold values from 0.5 to 1.5
- shift_two: float32 [768], replicated, may hold values from -3 to 3
- cotangent: bfloat16 [16, 512, 768], P('dp'), may hold values from -6 to 6
Outputs:
- layer_out: bfloat16 [16, 512, 768], P('dp')
- grad_tokens: float32 [16, 512, 768], P('dp')
- grad_w_qkv: float32 [3, 768, 768], P(None, None, 'mp')
- grad_w_pos: float32 [2, 768, 768], P(None, None, 'mp')
- grad_w_out: float32 [768, 768], P('mp')
- grad_b_out: float32 [768], replicated
- grad_gain_one: float32 [768], replicated
- grad_shift_one: float32 [768], replicated
- grad_w_in: float32 [768, 3072], P(None, 'mp')
- grad_b_in: float32 [3072], P('mp')
- grad_w_back: float32 [3072, 768], P('mp')
- grad_b_back: float32 [768], replicated
- grad_gain_two: float32 [768], replicated
- grad_shift_two: float32 [768], replicated
Inputs may be any that keep to these rules, and one draw needn't show every extreme that they name: `lengths`: in every draw some page has all 512 tokens real.
All inputs are finite; a program needn't handle non-finite values.
Results may differ from a plain program's by a relative error of at most 0.015.
Values sent between devices are 32-bit elements; how exact they have to be, the bound alone decides.
No kernel may reach another device: no remote copies, remote signals or barrier semaphores. Data moves between devices by JAX's collectives and lax.ppermute only.
A program may use at most 128 MiB of HBM per device.

v0:
```python
from functools import partial
import math
import jax
import jax.numpy as jnp
from jax import lax
from jax.sharding import PartitionSpec as P

HEAD_DIM = 64


def sinusoid(coords, model_width):
    quarter = model_width // 4
    frequency = jnp.exp(jnp.arange(quarter, dtype=jnp.float32) * (-math.log(10000.0) / quarter))
    position = coords.astype(jnp.float32)
    phases = position[:, :, None] * frequency
    sin_cos = jnp.concatenate([jnp.sin(phases), jnp.cos(phases)], axis=2)
    return jnp.concatenate([sin_cos[0], sin_cos[1]], axis=1)


def layer_norm(values, norm_gain, norm_shift):
    center = values - jnp.mean(values, axis=-1, keepdims=True)
    spread = jnp.mean(center * center, axis=-1, keepdims=True)
    return center * lax.rsqrt(spread + 1e-05) * norm_gain + norm_shift


def exact_gelu(values):
    return jax.nn.gelu(values, approximate=False)


def page_scores(queries, key_rows, pos_query, pos_key, page_length):
    factor = 1.0 / math.sqrt(3.0 * queries.shape[2])
    scores = jnp.einsum("ihd,jhd->hij", queries, key_rows, preferred_element_type=jnp.float32)
    scores = scores + jnp.einsum(
        "ihd,jhd->hij", queries, pos_key, preferred_element_type=jnp.float32
    )
    scores = scores + jnp.einsum(
        "ihd,jhd->hij", pos_query, key_rows, preferred_element_type=jnp.float32
    )
    scores = scores * factor
    visible = jnp.arange(queries.shape[0]) < page_length
    return jnp.where(visible[None, None, :], scores, -1e30)


def attend_page(inputs):
    queries, key_rows, value_rows, pos_query, pos_key, page_length = inputs
    scores = page_scores(queries, key_rows, pos_query, pos_key, page_length)
    highest = jnp.max(scores, axis=2, keepdims=True)
    totals = jnp.sum(jnp.exp(scores - highest), axis=2, keepdims=True)
    log_total = highest + jnp.log(totals)
    weights = jnp.exp(scores - log_total).astype(jnp.bfloat16)
    mixed = jnp.einsum("hij,jhd->ihd", weights, value_rows, preferred_element_type=jnp.float32)
    return (mixed.astype(jnp.bfloat16), log_total)


def page_backward(inputs):
    queries, key_rows, value_rows, pos_query, pos_key, page_length, log_total, d_mixed = inputs
    factor = 1.0 / math.sqrt(3.0 * queries.shape[2])
    scores = page_scores(queries, key_rows, pos_query, pos_key, page_length)
    probs = jnp.exp(scores - log_total)
    weights = probs.astype(jnp.bfloat16)
    d_values = jnp.einsum("hij,ihd->jhd", weights, d_mixed, preferred_element_type=jnp.float32)
    d_probs = jnp.einsum("ihd,jhd->hij", d_mixed, value_rows, preferred_element_type=jnp.float32)
    d_scores = (probs * (d_probs - jnp.sum(d_probs * probs, axis=2, keepdims=True))).astype(
        jnp.bfloat16
    )
    by_key = jnp.einsum("hij,jhd->ihd", d_scores, key_rows, preferred_element_type=jnp.float32)
    by_pos_key = jnp.einsum("hij,jhd->ihd", d_scores, pos_key, preferred_element_type=jnp.float32)
    by_query = jnp.einsum("hij,ihd->jhd", d_scores, queries, preferred_element_type=jnp.float32)
    by_pos_query = jnp.einsum(
        "hij,ihd->jhd", d_scores, pos_query, preferred_element_type=jnp.float32
    )
    d_queries = ((by_key + by_pos_key) * factor).astype(jnp.bfloat16)
    d_pos_query = (by_key * factor).astype(jnp.bfloat16)
    d_keys = ((by_query + by_pos_query) * factor).astype(jnp.bfloat16)
    d_pos_key = (by_query * factor).astype(jnp.bfloat16)
    return (d_queries, d_keys, d_values.astype(jnp.bfloat16), d_pos_query, d_pos_key)


def forward(
    token_rows,
    position,
    lengths,
    w_qkv,
    w_pos,
    w_out,
    b_out,
    gain_one,
    shift_one,
    w_in,
    b_in,
    w_back,
    b_back,
    gain_two,
    shift_two,
):
    page_count = lengths.shape[0]
    page_len = token_rows.shape[0] // page_count
    heads_here = w_qkv.shape[2] // HEAD_DIM

    def split_heads(values):
        return values.astype(jnp.bfloat16).reshape(page_count, page_len, heads_here, HEAD_DIM)

    queries = split_heads(jnp.dot(token_rows, w_qkv[0], preferred_element_type=jnp.float32))
    key_rows = split_heads(jnp.dot(token_rows, w_qkv[1], preferred_element_type=jnp.float32))
    value_rows = split_heads(jnp.dot(token_rows, w_qkv[2], preferred_element_type=jnp.float32))
    pos_query = split_heads(jnp.dot(position, w_pos[0], preferred_element_type=jnp.float32))
    pos_key = split_heads(jnp.dot(position, w_pos[1], preferred_element_type=jnp.float32))
    mixed, log_total = lax.map(
        attend_page, (queries, key_rows, value_rows, pos_query, pos_key, lengths)
    )
    mixed = mixed.reshape(page_count * page_len, heads_here * HEAD_DIM)
    branch = lax.psum(jnp.dot(mixed, w_out, preferred_element_type=jnp.float32), "mp") + b_out
    first = token_rows.astype(jnp.float32) + branch
    normed = layer_norm(first, gain_one, shift_one)
    normed_low = normed.astype(jnp.bfloat16)
    hidden_pre = jnp.dot(normed_low, w_in, preferred_element_type=jnp.float32) + b_in
    hidden = exact_gelu(hidden_pre).astype(jnp.bfloat16)
    feed = lax.psum(jnp.dot(hidden, w_back, preferred_element_type=jnp.float32), "mp") + b_back
    second = normed + feed
    output = layer_norm(second, gain_two, shift_two)
    saved = (
        queries,
        key_rows,
        value_rows,
        pos_query,
        pos_key,
        mixed,
        log_total,
        first,
        normed,
        normed_low,
        hidden_pre,
        hidden,
        second,
    )
    return (output, saved)


def body(
    tokens,
    lengths,
    coords,
    w_qkv,
    w_pos,
    w_out,
    b_out,
    gain_one,
    shift_one,
    w_in,
    b_in,
    w_back,
    b_back,
    gain_two,
    shift_two,
    cotangent,
):
    page_count, page_len, model_width = tokens.shape
    token_rows = tokens.reshape(page_count * page_len, model_width)
    position = jax.vmap(partial(sinusoid, model_width=model_width))(coords)
    position = position.astype(jnp.bfloat16).reshape(page_count * page_len, model_width)
    weights_all = (
        w_qkv,
        w_pos,
        w_out,
        b_out,
        gain_one,
        shift_one,
        w_in,
        b_in,
        w_back,
        b_back,
        gain_two,
        shift_two,
    )
    output, saved = forward(token_rows, position, lengths, *weights_all)
    (
        queries,
        key_rows,
        value_rows,
        pos_query,
        pos_key,
        mixed,
        log_total,
        first,
        normed,
        normed_low,
        hidden_pre,
        hidden,
        second,
    ) = saved
    heads_here = w_qkv.shape[2] // HEAD_DIM
    d_output = cotangent.reshape(page_count * page_len, model_width).astype(jnp.float32)
    unused_two, pull_two = jax.vjp(layer_norm, second, gain_two, shift_two)
    d_second, d_gain_two, d_shift_two = pull_two(d_output)
    d_feed = d_second.astype(jnp.bfloat16)
    d_b_back = jnp.sum(d_feed.astype(jnp.float32), axis=0)
    d_w_back = jnp.dot(hidden.T, d_feed, preferred_element_type=jnp.float32)
    d_hidden = jnp.dot(d_feed, w_back.T, preferred_element_type=jnp.float32)
    unused_gelu, pull_gelu = jax.vjp(exact_gelu, hidden_pre)
    d_pre = pull_gelu(d_hidden)[0].astype(jnp.bfloat16)
    d_b_in = jnp.sum(d_pre.astype(jnp.float32), axis=0)
    d_w_in = jnp.dot(normed_low.T, d_pre, preferred_element_type=jnp.float32)
    ffn_terms = (d_w_in, d_b_in, d_w_back, d_b_back, d_gain_two, d_shift_two)
    d_normed = d_second + lax.psum(jnp.dot(d_pre, w_in.T, preferred_element_type=jnp.float32), "mp")
    unused_one, pull_one = jax.vjp(layer_norm, first, gain_one, shift_one)
    d_first, d_gain_one, d_shift_one = pull_one(d_normed)
    d_branch = d_first.astype(jnp.bfloat16)
    d_b_out = jnp.sum(d_branch.astype(jnp.float32), axis=0)
    d_w_out = jnp.dot(mixed.T, d_branch, preferred_element_type=jnp.float32)
    d_mixed = jnp.dot(d_branch, w_out.T, preferred_element_type=jnp.float32).astype(jnp.bfloat16)
    d_mixed = d_mixed.reshape(page_count, page_len, heads_here, HEAD_DIM)
    head_grads = lax.map(
        page_backward,
        (queries, key_rows, value_rows, pos_query, pos_key, lengths, log_total, d_mixed),
    )
    flat_grads = [
        piece.reshape(page_count * page_len, heads_here * HEAD_DIM) for piece in head_grads
    ]
    d_queries, d_keys, d_values, d_pos_query, d_pos_key = flat_grads
    d_w_qkv = jnp.stack(
        [
            jnp.dot(token_rows.T, d_queries, preferred_element_type=jnp.float32),
            jnp.dot(token_rows.T, d_keys, preferred_element_type=jnp.float32),
            jnp.dot(token_rows.T, d_values, preferred_element_type=jnp.float32),
        ]
    )
    d_w_pos = jnp.stack(
        [
            jnp.dot(position.T, d_pos_query, preferred_element_type=jnp.float32),
            jnp.dot(position.T, d_pos_key, preferred_element_type=jnp.float32),
        ]
    )
    input_part = jnp.dot(d_queries, w_qkv[0].T, preferred_element_type=jnp.float32)
    input_part = input_part + jnp.dot(d_keys, w_qkv[1].T, preferred_element_type=jnp.float32)
    input_part = input_part + jnp.dot(d_values, w_qkv[2].T, preferred_element_type=jnp.float32)
    d_tokens = d_first + lax.psum(input_part, "mp")
    summed = lax.psum(
        (
            d_w_qkv,
            d_w_pos,
            d_w_out,
            d_b_out,
            d_gain_one,
            d_shift_one,
            d_w_in,
            d_b_in,
            d_w_back,
            d_b_back,
            d_gain_two,
            d_shift_two,
        ),
        "dp",
    )
    attn_terms = summed[:6]
    ffn_terms = summed[6:]
    sum_w_qkv, sum_w_pos, sum_w_out, sum_b_out, sum_gain_one, sum_shift_one = attn_terms
    sum_w_in, sum_b_in, sum_w_back, sum_b_back, sum_gain_two, sum_shift_two = ffn_terms
    layer_out = output.astype(jnp.bfloat16).reshape(page_count, page_len, model_width)
    grad_tokens = d_tokens.reshape(page_count, page_len, model_width)
    return (
        layer_out,
        grad_tokens,
        sum_w_qkv,
        sum_w_pos,
        sum_w_out,
        sum_b_out,
        sum_gain_one,
        sum_shift_one,
        sum_w_in,
        sum_b_in,
        sum_w_back,
        sum_b_back,
        sum_gain_two,
        sum_shift_two,
    )


def solution(mesh):
    placed = (
        P("dp", None, None),
        P("dp"),
        P("dp", None, None),
        P(None, None, "mp"),
        P(None, None, "mp"),
        P("mp", None),
        P(),
        P(),
        P(),
        P(None, "mp"),
        P("mp"),
        P("mp", None),
        P(),
        P(),
        P(),
        P("dp", None, None),
    )
    return jax.shard_map(
        body,
        mesh=mesh,
        in_specs=placed,
        out_specs=(
            P("dp", None, None),
            P("dp", None, None),
            P(None, None, "mp"),
            P(None, None, "mp"),
            P("mp", None),
            P(),
            P(),
            P(),
            P(None, "mp"),
            P("mp"),
            P("mp", None),
            P(),
            P(),
            P(),
        ),
        check_vma=False,
    )
```

profile of v0, /device:TPU:0, one launch (start us, length us, event | category | flops | bytes accessed | tf_op | source)
XLA Modules:
  0.0 760.1 jit_solution(17825696523205868860)
XLA Ops:
  7.8 2.9 convolution_convert_fusion.3
  14.5 8.2 %multiply_sine_fusion = (bf16[2,2,512,192]{3,2,1,0:T(8,128)(2,1)S(1)}, bf16[2,2,512,192]{3,2,1,0:T(8,128)(2,1)S(1)}) fusion(f32[192]{0:T(256)S(1)} %copy-done.47, f32[2,2,512]{2,1,0:T(2,128)S(1)} %convert_element_type.111), kind=kLoop, calls=%fused_computation.137 | loop fusion | flops 1179648 | bytes 1581824 | tf_op jit(solution)/shard_map/vmap()/sin | solution.py:16
  30.4 10.8 %while.30 = (s32[]{:T(128)}, bf16[2,512,3,64]{1,3,2,0:T(8,128)(2,1)S(1)}, f32[2,3,512,1]{2,1,3,0:T(4,128)S(1)}, bf16[2,512,3,64]{1,3,2,0:T(8,128)(2,1)S(1)}, s32...) while((s32[]{:T(128)}, ...), condition=%wide.region_3.4_spmd, body=%wide.region_0.3_spmd.sunk | while | flops 409828352 | bytes 23657600 | solution.py:108
  41.7 3.3 fusion.129
  45.5 123.4 %all-reduce.8.cloned.1.call-done = f32[1024,768]{1,0:T(8,128)} async-done(((f32[1024,768]{1,0:T(8,128)}), f32[1024,768]{1,0:T(8,128)}) %all-reduce.8.cloned.1.call-update) | async-done | bytes 3145744 | tf_op jit(solution)/shard_map/psum | solution.py:112
  168.9 2.8 fusion.123
  173.3 9.6 %multiply_convert_fusion.3 = (bf16[1024,768]{1,0:T(8,128)(2,1)S(1)}, f32[1024,768]{1,0:T(8,128)}, f32[1024,768]{1,0:T(8,128)}) fusion(f32[768]{0:T(1024)S(1)} %copy-done.51, bf16[768,768]{1,0:T(8,128)(2,1)S(1)} %copy-done, f32[1024,768]{1,0:T(8,128)S(1)} %get-tuple-element.272, f32[768]{0:T(1024)S(1)} %copy-done.44, f32[768]{0:T(1024)S(1)} %copy-done.32, ...), kind=kOutput, calls=%fused_computation.119 | convolution fusion | flops 1263796224 | bytes 12207104 | tf_op jit(solution)/shard_map/dot_general | solution.py:116
  184.1 3.1 fusion.130
  187.3 120.2 %all-reduce.10.cloned.1.call-done = f32[1024,768]{1,0:T(8,128)} async-done(((f32[1024,768]{1,0:T(8,128)}), f32[1024,768]{1,0:T(8,128)}) %all-reduce.10.cloned.1.call-update) | async-done | bytes 3145744 | tf_op jit(solution)/shard_map/psum | solution.py:118
  307.5 3.9 fusion.121
  314.5 2.6 fusion.120
  320.5 2.8 convert_reduce_fusion.2
  324.5 3.1 fusion.131
  327.9 120.0 %all-reduce.12.cloned.1.call-done = f32[1024,768]{1,0:T(8,128)} async-done(((f32[1024,768]{1,0:T(8,128)}), f32[1024,768]{1,0:T(8,128)}) %all-reduce.12.cloned.1.call-update) | async-done | bytes 3145744 | tf_op jit(solution)/shard_map/psum | solution.py:204
  447.9 5.2 multiply_reduce_fusion.1
  453.1 2.8 fusion.119
  463.9 22.3 %while.31 = (s32[]{:T(128)}, bf16[2,512,3,64]{1,3,2,0:T(8,128)(2,1)}, bf16[2,512,3,64]{1,3,2,0:T(8,128)(2,1)}, bf16[2,512,3,64]{1,3,2,0:T(8,128)(2,1)}, bf16[2,5...) while((s32[]{:T(128)}, ...), condition=%wide.region_17.18_spmd, body=%wide.region_15.17_spmd.sunk | while | flops 915700736 | bytes 53913936 | solution.py:212
  494.5 4.9 fusion.133
  499.4 3.3 fusion.126
  512.0 26.2 %all-reduce = (f32[768]{0:T(1024)}, f32[768]{0:T(1024)}, f32[768]{0:T(1024)}, f32[768]{0:T(1024)}, f32[768]{0:T(1024)}, /*index=5*/f32[768]{0:T(1024)}, f32[768]{0:T(1024)}) all-reduce(f32[768]{0:T(1024)S(1)} %copy-done.38, f32[768]{0:T(1024)S(1)} %copy-done.35, f32[768]{0:T(1024)S(1)} %copy-done.36, ...), channel_id=1, replica_groups=mesh['dp'=8,'mp'=4] {'dp'}, use_global_device_ids=true, to_apply=%region_23.24 | all-reduce | flops 5376 | bytes 43008 | tf_op jit(solution)/shard_map/psum | solution.py:237
  538.2 76.3 %all-reduce.14.cloned.1.call-done = f32[1024,768]{1,0:T(8,128)} async-done(((f32[1024,768]{1,0:T(8,128)}), f32[1024,768]{1,0:T(8,128)}) %all-reduce.14.cloned.1.call-update) | async-done | bytes 3145744 | tf_op jit(solution)/shard_map/psum | solution.py:236
  614.5 4.9 add_add_fusion.5
  619.3 126.4 %all-reduce.16.cloned.1.call-done = (f32[3,768,192]{1,2,0:T(8,128)}, f32[2,768,192]{1,2,0:T(8,128)}, f32[192,768]{1,0:T(8,128)}, f32[768,768]{1,0:T(8,128)}, f32[768,768]{1,0:T(8,128)}) async-done(((f32[3,768,192]{1,2,0:T(8,128)}, f32[2,768,192]{1,2,0:T(8,128)}, f32[192,768]{1,0:T(8,128)}, f32[768,768]{1,0:T(8,128)}, f32[768,768]{1,0:T(8,128)}), (f32[3,768,192]{1,2,0:T(8,128)}, f32[2,768,192]{1,2,0:T(8,128)}, ...) | async-done | bytes 8257552 | tf_op jit(solution)/shard_map/psum | solution.py:237
  745.7 2.9 copy.127
  (249 shorter events, 86.2 us)
Async XLA Ops:
  7.2 166.1 %copy-start = (bf16[768,768]{1,0:T(8,128)(2,1)S(1)}, bf16[768,768]{1,0:T(8,128)(2,1)}, u32[]{:S(2)}) copy-start(bf16[768,768]{1,0:T(8,128)(2,1)} %param.29) | copy-start | bytes 3538948
  7.2 5.7 copy-start.6
  7.2 161.7 %all-reduce.8.cloned.1.call-start = ((), (), s32[]{:S(2)}) async-start(), calls=%async_computation | async-start | bytes 6291456 | tf_op jit(solution)/shard_map/psum | solution.py:112
  7.8 6.7 copy-start.41
  7.8 6.7 copy-start.47
  41.2 3.8 copy-start.31
  45.0 262.5 %all-reduce.10.cloned.1.call-start = ((), (), s32[]{:S(2)}) async-start(), calls=%async_computation.1 | async-start | bytes 6291456 | tf_op jit(solution)/shard_map/psum | solution.py:118
  171.7 11.2 %copy-start.2 = (f32[1024,768]{1,0:T(8,128)}, f32[1024,768]{1,0:T(8,128)S(1)}, u32[]{:S(2)}) copy-start(f32[1024,768]{1,0:T(8,128)S(1)} %get-tuple-element.272) | copy-start | bytes 9437188
  173.3 10.8 %copy-start.48 = (bf16[768,768]{1,0:T(8,128)(2,1)S(1)}, bf16[768,768]{1,0:T(8,128)(2,1)}, u32[]{:S(2)}) copy-start(bf16[768,768]{1,0:T(8,128)(2,1)} %param.31) | copy-start | bytes 3538948
  187.2 120.3 %copy-start.42 = (f32[768]{0:T(1024)S(1)}, f32[768]{0:T(1024)}, u32[]{:S(2)}) copy-start(f32[768]{0:T(1024)} %param.32) | copy-start | bytes 9220
  187.2 260.7 %all-reduce.12.cloned.1.call-start = ((), (), s32[]{:S(2)}) async-start(), calls=%async_computation.2 | async-start | bytes 6291456 | tf_op jit(solution)/shard_map/psum | solution.py:204
  314.5 5.2 copy-start.57
  319.8 3.6 copy-start.21
  327.6 125.5 %copy-start.34 = (f32[1024]{0:T(1024)S(1)}, f32[1024]{0:T(1024)}, u32[]{:S(2)}) copy-start(f32[1024]{0:T(1024)} %copy-done.33) | copy-start | bytes 12292
  327.6 286.8 %all-reduce.14.cloned.1.call-start = ((), (), s32[]{:S(2)}) async-start(), calls=%async_computation.3 | async-start | bytes 6291456 | tf_op jit(solution)/shard_map/psum | solution.py:236
  456.0 3.8 copy-start.30
  486.2 4.5 copy-start.23
  494.2 5.2 copy-start.45
  494.2 251.5 %all-reduce.16.cloned.1.call-start = ((), (), s32[]{:S(2)}) async-start(), calls=%async_computation.4 | async-start | bytes 16515072 | tf_op jit(solution)/shard_map/psum | solution.py:237
  494.5 4.9 copy-start.3
  494.5 4.9 copy-start.55
  499.4 3.8 copy-start.16
  745.7 4.0 copy-start.28
  745.7 4.8 copy-start.13
  (45 other events, 72.8 us)
Sparse Core Ops, SparseCore 0:
  45.1 123.7 all-reduce.7
  187.3 120.0 all-reduce.9
  327.8 120.0 all-reduce.11
  494.3 120.0 all-reduce.13
  619.9 125.7 all-reduce.15
where the time goes:
time: 768 us; the launch traced here: 760 us
  waiting for transfers between devices  566 us (74%)
  matrix products  66.3 us (9%)
  other arithmetic  44.3 us (6%)
  local copies, waits for them, and re-layouts  40.9 us (5%)
  blocking collectives  26.2 us (3%)
  between operations  14.7 us (2%)
    psum x1, waiting for transfers between devices, body(): lax.psum((d_w_qkv, d_w_pos, d_w_out, d_b_out, d_gain_one, d_shift_one, d_...  126 us
    psum x1, waiting for transfers between devices, forward(): lax.psum(jnp.dot(mixed, w_out, preferred_element_type=jnp.float32), 'mp')  123 us
    psum x1, waiting for transfers between devices, forward(): lax.psum(jnp.dot(hidden, w_back, preferred_element_type=jnp.float32), 'mp')  120 us
    psum x1, waiting for transfers between devices, body(): lax.psum(jnp.dot(d_pre, w_in.T, preferred_element_type=jnp.float32), 'mp')  120 us
    psum x1, waiting for transfers between devices, body(): d_tokens = d_first + lax.psum(input_part, 'mp')  76.3 us
    psum x1, blocking collectives, body(): lax.psum((d_w_qkv, d_w_pos, d_w_out, d_b_out, d_gain_one, d_shift_one, d_...  26.2 us
    unnamed x115, local copies, waits for them, and re-layouts  19.5 us
  transfers between devices with their start and end apart: 5, of which 5 were waited for; matrix products, arithmetic and copies ran while one was open for 3% of the time, Pallas kernels for 0%

commit v1 on v0

--- a/solution.py
+++ b/solution.py
@@ -6,6 +6,12 @@
 from jax.sharding import PartitionSpec as P
 
 HEAD_DIM = 64
+
+
+def summed_here(x, axis):
+    parts = lax.all_gather(x, axis, axis=0, tiled=False)
+    total = parts.sum(axis=0)
+    return total
 
 
 def sinusoid(coords, model_width):
@@ -233,7 +239,7 @@
     input_part = jnp.dot(d_queries, w_qkv[0].T, preferred_element_type=jnp.float32)
     input_part = input_part + jnp.dot(d_keys, w_qkv[1].T, preferred_element_type=jnp.float32)
     input_part = input_part + jnp.dot(d_values, w_qkv[2].T, preferred_element_type=jnp.float32)
-    d_tokens = d_first + lax.psum(input_part, "mp")
+    d_tokens = d_first + summed_here(input_part, "mp")
     summed = lax.psum(
         (
             d_w_qkv,

time: 768 us -> 864 us (1.12)
  waiting for transfers between devices: 566 us -> 654 us
    all_gather x0 -> x1, waiting for transfers between devices: none -> 173 us  [summed_here(): parts = lax.all_gather(x, axis, axis=0, tiled=False)]
    psum x1 -> x0, waiting for transfers between devices: 76.3 us -> none  [body(): d_tokens = d_first + lax.psum(input_part, 'mp')]
    psum x1, waiting for transfers between devices: 126 us -> 117 us  [body(): lax.psum((d_w_qkv, d_w_pos, d_w_out, d_b_out, d_gain_one, d_shift_one, d_...]
where the time goes in v1:
time: 864 us; the launch traced here: 856 us
  waiting for transfers between devices  654 us (76%)
  matrix products  66.3 us (8%)
  other arithmetic  52.4 us (6%)
  local copies, waits for them, and re-layouts  41.1 us (5%)
  blocking collectives  26.2 us (3%)
  between operations  14.7 us (2%)
    all_gather x1, waiting for transfers between devices, summed_here(): parts = lax.all_gather(x, axis, axis=0, tiled=False)  173 us
    psum x1, waiting for transfers between devices, forward(): lax.psum(jnp.dot(mixed, w_out, preferred_element_type=jnp.float32), 'mp')  123 us
    psum x1, waiting for transfers between devices, forward(): lax.psum(jnp.dot(hidden, w_back, preferred_element_type=jnp.float32), 'mp')  120 us
    psum x1, waiting for transfers between devices, body(): lax.psum(jnp.dot(d_pre, w_in.T, preferred_element_type=jnp.float32), 'mp')  120 us
    psum x1, waiting for transfers between devices, body(): lax.psum((d_w_qkv, d_w_pos, d_w_out, d_b_out, d_gain_one, d_shift_one, d_...  117 us
    psum x1, blocking collectives, body(): lax.psum((d_w_qkv, d_w_pos, d_w_out, d_b_out, d_gain_one, d_shift_one, d_...  26.2 us
    unnamed x115, local copies, waits for them, and re-layouts  19.7 us
  transfers between devices with their start and end apart: 5, of which 5 were waited for; matrix products, arithmetic and copies ran while one was open for 3% of the time, Pallas kernels for 0%

profile of v1, /device:TPU:0, one launch (start us, length us, event | category | flops | bytes accessed | tf_op | source)
XLA Modules:
  0.0 856.2 jit_solution(14313444498328438055)
XLA Ops:
  7.8 2.9 convolution_convert_fusion.3
  14.5 8.2 multiply_sine_fusion
  30.4 10.8 %while.30 = (s32[]{:T(128)}, bf16[2,512,3,64]{1,3,2,0:T(8,128)(2,1)S(1)}, f32[2,3,512,1]{2,1,3,0:T(4,128)S(1)}, bf16[2,512,3,64]{1,3,2,0:T(8,128)(2,1)S(1)}, s32...) while((s32[]{:T(128)}, ...), condition=%wide.region_3.4_spmd, body=%wide.region_0.3_spmd.sunk | while | flops 409828352 | bytes 23657600 | solution.py:114
  41.7 3.3 fusion.129
  45.5 123.4 %all-reduce.7.cloned.1.call-done = f32[1024,768]{1,0:T(8,128)} async-done(((f32[1024,768]{1,0:T(8,128)}), f32[1024,768]{1,0:T(8,128)}) %all-reduce.7.cloned.1.call-update) | async-done | bytes 3145744 | tf_op jit(solution)/shard_map/psum | solution.py:118
  168.9 2.8 fusion.123
  173.3 9.6 %multiply_convert_fusion.3 = (bf16[1024,768]{1,0:T(8,128)(2,1)S(1)}, f32[1024,768]{1,0:T(8,128)}, f32[1024,768]{1,0:T(8,128)}) fusion(f32[768]{0:T(1024)S(1)} %copy-done.51, bf16[768,768]{1,0:T(8,128)(2,1)S(1)} %copy-done, f32[1024,768]{1,0:T(8,128)S(1)} %get-tuple-element.272, f32[768]{0:T(1024)S(1)} %copy-done.44, f32[768]{0:T(1024)S(1)} %copy-done.32, ...), kind=kOutput, calls=%fused_computation.119 | convolution fusion | flops 1263796224 | bytes 12207104 | tf_op jit(solution)/shard_map/dot_general | solution.py:122
  184.1 3.1 fusion.130
  187.3 120.2 %all-reduce.9.cloned.1.call-done = f32[1024,768]{1,0:T(8,128)} async-done(((f32[1024,768]{1,0:T(8,128)}), f32[1024,768]{1,0:T(8,128)}) %all-reduce.9.cloned.1.call-update) | async-done | bytes 3145744 | tf_op jit(solution)/shard_map/psum | solution.py:124
  307.5 3.9 fusion.121
  320.6 2.8 convert_reduce_fusion.2
  324.5 3.1 fusion.131
  327.9 120.0 %all-reduce.11.cloned.1.call-done = f32[1024,768]{1,0:T(8,128)} async-done(((f32[1024,768]{1,0:T(8,128)}), f32[1024,768]{1,0:T(8,128)}) %all-reduce.11.cloned.1.call-update) | async-done | bytes 3145744 | tf_op jit(solution)/shard_map/psum | solution.py:210
  447.9 5.2 multiply_reduce_fusion.1
  453.1 2.8 fusion.119
  463.9 22.1 %while.31 = (s32[]{:T(128)}, bf16[2,512,3,64]{1,3,2,0:T(8,128)(2,1)}, bf16[2,512,3,64]{1,3,2,0:T(8,128)(2,1)}, bf16[2,512,3,64]{1,3,2,0:T(8,128)(2,1)}, bf16[2,5...) while((s32[]{:T(128)}, ...), condition=%wide.region_17.18_spmd, body=%wide.region_15.17_spmd.sunk | while | flops 915700736 | bytes 53913936 | solution.py:218
  494.3 4.9 fusion.133
  499.2 3.3 fusion.126
  512.1 26.2 %all-reduce = (f32[768]{0:T(1024)}, f32[768]{0:T(1024)}, f32[768]{0:T(1024)}, f32[768]{0:T(1024)}, f32[768]{0:T(1024)}, /*index=5*/f32[768]{0:T(1024)}, f32[768]{0:T(1024)}) all-reduce(f32[768]{0:T(1024)S(1)} %copy-done.38, f32[768]{0:T(1024)S(1)} %copy-done.35, f32[768]{0:T(1024)S(1)} %copy-done.36, ...), channel_id=1, replica_groups=mesh['dp'=8,'mp'=4] {'dp'}, use_global_device_ids=true, to_apply=%region_23.24 | all-reduce | flops 5376 | bytes 43008 | tf_op jit(solution)/shard_map/psum | solution.py:243
  538.3 173.1 %all-gather.3.cloned.1.call-done = f32[4096,768]{1,0:T(8,128)} async-done(((f32[1024,768]{1,0:T(8,128)}), f32[4096,768]{1,0:T(8,128)}) %all-gather.3.cloned.1.call-update) | async-done | bytes 12582928 | tf_op jit(solution)/shard_map/all_gather | solution.py:12
  711.4 7.5 reduce_sum.171
  718.9 5.6 add_add_fusion.5
  724.5 117.3 %all-reduce.13.cloned.1.call-done = (f32[3,768,192]{1,2,0:T(8,128)}, f32[2,768,192]{1,2,0:T(8,128)}, f32[192,768]{1,0:T(8,128)}, f32[768,768]{1,0:T(8,128)}, f32[768,768]{1,0:T(8,128)}) async-done(((f32[3,768,192]{1,2,0:T(8,128)}, f32[2,768,192]{1,2,0:T(8,128)}, f32[192,768]{1,0:T(8,128)}, f32[768,768]{1,0:T(8,128)}, f32[768,768]{1,0:T(8,128)}), (f32[3,768,192]{1,2,0:T(8,128)}, f32[2,768,192]{1,2,0:T(8,128)}, ...) | async-done | bytes 8257552 | tf_op jit(solution)/shard_map/psum | solution.py:243
  841.8 2.9 copy.126
  (250 shorter events, 88.9 us)
Async XLA Ops:
  7.2 166.1 %copy-start = (bf16[768,768]{1,0:T(8,128)(2,1)S(1)}, bf16[768,768]{1,0:T(8,128)(2,1)}, u32[]{:S(2)}) copy-start(bf16[768,768]{1,0:T(8,128)(2,1)} %param.29) | copy-start | bytes 3538948
  7.2 5.7 copy-start.6
  7.2 161.7 %all-reduce.7.cloned.1.call-start = ((), (), s32[]{:S(2)}) async-start(), calls=%async_computation | async-start | bytes 6291456 | tf_op jit(solution)/shard_map/psum | solution.py:118
  7.8 6.7 copy-start.41
  7.8 6.7 copy-start.47
  41.2 3.8 copy-start.31
  45.0 262.5 %all-reduce.9.cloned.1.call-start = ((), (), s32[]{:S(2)}) async-start(), calls=%async_computation.1 | async-start | bytes 6291456 | tf_op jit(solution)/shard_map/psum | solution.py:124
  171.7 11.2 %copy-start.2 = (f32[1024,768]{1,0:T(8,128)}, f32[1024,768]{1,0:T(8,128)S(1)}, u32[]{:S(2)}) copy-start(f32[1024,768]{1,0:T(8,128)S(1)} %get-tuple-element.272) | copy-start | bytes 9437188
  173.3 10.8 %copy-start.48 = (bf16[768,768]{1,0:T(8,128)(2,1)S(1)}, bf16[768,768]{1,0:T(8,128)(2,1)}, u32[]{:S(2)}) copy-start(bf16[768,768]{1,0:T(8,128)(2,1)} %param.31) | copy-start | bytes 3538948
  187.2 120.3 %copy-start.42 = (f32[768]{0:T(1024)S(1)}, f32[768]{0:T(1024)}, u32[]{:S(2)}) copy-start(f32[768]{0:T(1024)} %param.32) | copy-start | bytes 9220
  187.2 260.7 %all-reduce.11.cloned.1.call-start = ((), (), s32[]{:S(2)}) async-start(), calls=%async_computation.2 | async-start | bytes 6291456 | tf_op jit(solution)/shard_map/psum | solution.py:210
  314.6 5.2 copy-start.57
  319.8 3.6 copy-start.21
  327.7 125.5 %copy-start.34 = (f32[1024]{0:T(1024)S(1)}, f32[1024]{0:T(1024)}, u32[]{:S(2)}) copy-start(f32[1024]{0:T(1024)} %copy-done.33) | copy-start | bytes 12292
  327.7 383.7 %all-gather.3.cloned.1.call-start = ((), (), s32[]{:S(2)}) async-start(), calls=%async_computation.3 | async-start | bytes 15728640 | tf_op jit(solution)/shard_map/all_gather | solution.py:12
  456.0 3.7 copy-start.30
  486.0 4.5 copy-start.23
  494.0 5.2 copy-start.45
  494.0 347.8 %all-reduce.13.cloned.1.call-start = ((), (), s32[]{:S(2)}) async-start(), calls=%async_computation.4 | async-start | bytes 16515072 | tf_op jit(solution)/shard_map/psum | solution.py:243
  494.3 4.9 copy-start.3
  494.3 4.9 copy-start.55
  499.2 3.8 copy-start.16
  841.8 4.0 copy-start.28
  841.8 4.8 copy-start.13
  (45 other events, 73.0 us)
Sparse Core Ops, SparseCore 0:
  45.1 123.7 all-reduce.6
  187.4 120.0 all-reduce.8
  327.8 120.0 all-reduce.10
  494.2 217.2 all-gather.2
  716.9 124.9 all-reduce.12
